TPU v7x, 32 devices: a whole 2x2x4 slice. The times are simulated.
32 devices in a mesh: dp: 4 (over x, core), ctx: 2 (over y), tp: 4 (over z).
Axes of the slice: x: 2, y: 2, z: 4, core: 2. Of those that a mesh axis runs over, the one named last changes fastest.
Arguments:
- out_grad: bfloat16 [4096, 4096], P(('dp', 'ctx', 'tp')), may hold values from -6 to 6
- expert_ids: int32 [4096, 1], P(('dp', 'ctx', 'tp')), may hold values from 0 to 3
- gate_weight: float32 [4096, 1], P(('dp', 'ctx', 'tp')), may hold values from 0.2 to 1
- hidden_saved: bfloat16 [4, 4, 256, 1536], P('dp', 'tp', None, 'ctx'), may hold values from -1 to 1
- down_weight: bfloat16 [4, 1536, 4096], P('tp', 'ctx'), may hold values from -0.15625 to 0.15625
Outputs:
- hidden_grad: bfloat16 [4, 4, 256, 1536], P('dp', 'tp', None, 'ctx')
- weight_grad: bfloat16 [4, 1536, 4096], P('tp', 'ctx', 'dp')
All inputs are finite; a program needn't handle non-finite values.
Results may differ from a plain program's by a relative error of at most 0.013.
Values may be sent and summed in bfloat16 or wider, within the bound.
A program may use at most 64 MiB of HBM per device.

v0:
```python
import jax
import jax.numpy as jnp
from jax import lax
from jax.sharding import PartitionSpec as P


def per_device(out_grad, expert_ids, gate_weight, hidden_saved, down_weight):
    experts = lax.axis_size("tp")
    width = out_grad.shape[1]
    slots_all = hidden_saved.shape[2]
    capacity = slots_all // (lax.axis_size("ctx") * experts)
    choice_rows = expert_ids[:, 0]
    onehot = (choice_rows[:, None] == jnp.arange(experts, dtype=jnp.int32)[None, :]).astype(
        jnp.int32
    )
    before = jnp.cumsum(onehot, axis=0) - onehot
    slot_index = jnp.sum(before * onehot, axis=1)
    target = jnp.arange(experts * capacity, dtype=jnp.int32)
    select = (
        (choice_rows[None, :] == (target // capacity)[:, None])
        & (slot_index[None, :] == (target % capacity)[:, None])
    ).astype(jnp.bfloat16)
    routed = (gate_weight * out_grad.astype(jnp.float32)).astype(jnp.bfloat16)
    outgoing = jnp.dot(select, routed, preferred_element_type=jnp.float32).astype(jnp.bfloat16)
    outgoing = outgoing.reshape(experts, capacity, width)
    incoming = lax.all_to_all(outgoing, "tp", split_axis=0, concat_axis=0, tiled=True)
    incoming = incoming.reshape(experts * capacity, width)
    weight = down_weight[0]
    saved_rows = hidden_saved[0, 0]
    group_rows = lax.all_gather(incoming, "ctx", axis=0, tiled=True)
    hidden_grad = jnp.einsum("rd,fd->rf", group_rows, weight, preferred_element_type=jnp.float32)
    partial_value = jnp.einsum(
        "rf,rd->fd", saved_rows, group_rows, preferred_element_type=jnp.float32
    )
    rounded = lax.optimization_barrier(partial_value.astype(jnp.bfloat16)).astype(jnp.float32)
    summed = lax.psum_scatter(rounded.astype(jnp.bfloat16), "dp", scatter_dimension=1, tiled=True)
    return (hidden_grad.astype(jnp.bfloat16)[None, None], summed[None])


def solution(mesh):
    placed = (
        P(("dp", "ctx", "tp"), None),
        P(("dp", "ctx", "tp"), None),
        P(("dp", "ctx", "tp"), None),
        P("dp", "tp", None, "ctx"),
        P("tp", "ctx", None),
    )
    return jax.shard_map(
        per_device,
        mesh=mesh,
        in_specs=placed,
        out_specs=(P("dp", "tp", None, "ctx"), P("tp", "ctx", "dp")),
        check_vma=False,
    )
```

profile of v0, /device:TPU:0, one launch (start us, length us, event | category | flops | bytes accessed | tf_op | source)
XLA Modules:
  0.0 149.7 jit_solution(14983220521151460498)
XLA Ops:
  7.2 0.0 copy-start
  7.2 0.0 all-gather.2.cloned.1.call-start
  7.2 0.8 fusion.11
  8.0 0.2 reduce_window_sum.11
  8.2 0.8 select_reduce_fusion
  9.0 1.7 %convolution_convert_fusion.1 = bf16[128,4096]{1,0:T(8,128)(2,1)S(1)} fusion(bf16[128,4096]{1,0:T(8,128)(2,1)} %param.5, f32[128]{0:T(128)} %bitcast.27, s32[128]{0:T(128)S(1)} %select_reduce_fusion, s32[128]{0:T(128)} %bitcast.26, s32[128]{0:T(128)S(1)} %get-tuple-element.4, s32[128]{0:T(128)S(1)} %get-tuple-element.5), kind=kOutput, calls=%fused_computation.4 | convolution fusion | flops 136364032 | bytes 2099712 | tf_op jit(solution)/shard_map/dot_general | solution.py:24
  10.8 32.0 %all_to_all.5 = bf16[4,32,4096]{2,1,0:T(8,128)(2,1)} all-to-all(bf16[4,32,4096]{2,1,0:T(8,128)(2,1)S(1)} %bitcast.22), channel_id=1, replica_groups=mesh['dp'=4,'ctx'=2,'tp'=4] {'tp'}, dimensions={0} | all-to-all | bytes 2097152 | tf_op jit(solution)/shard_map/all_to_all | solution.py:26
  42.8 0.0 all-gather.2.cloned.1.call-update
  42.8 0.0 reduce-scatter.2.cloned.1.call-start
  42.8 32.3 %all-gather.2.cloned.1.call-done = bf16[256,4096]{1,0:T(8,128)(2,1)} async-done(((bf16[128,4096]{1,0:T(8,128)(2,1)}), bf16[256,4096]{1,0:T(8,128)(2,1)}) %all-gather.2.cloned.1.call-update) | async-done | bytes 2097168 | tf_op jit(solution)/shard_map/all_gather | solution.py:30
  75.1 0.0 copy-done
  75.1 6.1 %fusion.2 = bf16[768,4096]{0,1:T(8,128)(2,1)} fusion(bf16[256,4096]{1,0:T(8,128)(2,1)} %all-gather.2.cloned.1.call-done, bf16[1,1,256,768]{3,2,1,0:T(8,128)(2,1)S(1)} %copy-done), kind=kOutput, calls=%fused_computation.3 | convolution fusion | flops 1613758464 | bytes 8781824 | tf_op jit(solution)/shard_map/rf,rd->fd/dot_general | solution.py:32
  81.3 0.0 copy-start.1
  81.3 0.0 reduce-scatter.2.cloned.1.call-update
  81.3 1.6 %copy-done.1 = bf16[256,4096]{1,0:T(8,128)(2,1)S(1)} copy-done((bf16[256,4096]{1,0:T(8,128)(2,1)S(1)}, bf16[256,4096]{1,0:T(8,128)(2,1)}, u32[]{:S(2)}) %copy-start.1) | copy-done | bytes 2097176
  82.9 5.4 %fusion.6 = bf16[1,1,256,768]{3,2,1,0:T(8,128)(2,1)} fusion(bf16[256,4096]{1,0:T(8,128)(2,1)S(1)} %copy-done.1, bf16[1,768,4096]{2,1,0:T(8,128)(2,1)} %param.9), kind=kOutput, calls=%fused_computation.7 | convolution fusion | flops 1610809344 | bytes 8781824 | tf_op jit(solution)/shard_map/rd,fd->rf/dot_general | solution.py:31
  88.2 52.1 %reduce-scatter.2.cloned.1.call-done = bf16[768,1024]{0,1:T(8,128)(2,1)} async-done(((bf16[768,4096]{0,1:T(8,128)(2,1)}), bf16[768,1024]{0,1:T(8,128)(2,1)}) %reduce-scatter.2.cloned.1.call-update) | async-done | bytes 1572880 | tf_op jit(solution)/shard_map/reduce_scatter | solution.py:36
  140.3 2.6 %copy.7 = bf16[1,768,1024]{2,1,0:T(8,128)(2,1)} copy(bf16[1,768,1024]{1,2,0:T(8,128)(2,1)} %bitcast.23) | data formatting | bytes 3145728
  (1 shorter events, 0.0 us)
Async XLA Ops:
  7.2 68.0 %copy-start = (bf16[1,1,256,768]{3,2,1,0:T(8,128)(2,1)S(1)}, bf16[1,1,256,768]{3,2,1,0:T(8,128)(2,1)}, u32[]{:S(2)}) copy-start(bf16[1,1,256,768]{3,2,1,0:T(8,128)(2,1)} %param.8) | copy-start | bytes 1179652
  7.2 68.0 %all-gather.2.cloned.1.call-start = ((), (), s32[]{:S(2)}) async-start(), calls=%async_computation.2 | async-start | bytes 3145728 | tf_op jit(solution)/shard_map/all_gather | solution.py:30
  42.8 97.5 %reduce-scatter.2.cloned.1.call-start = ((), (), s32[]{:S(2)}) async-start(), calls=%async_computation.3 | async-start | bytes 7864320 | tf_op jit(solution)/shard_map/reduce_scatter | solution.py:36
  81.3 1.6 %copy-start.1 = (bf16[256,4096]{1,0:T(8,128)(2,1)S(1)}, bf16[256,4096]{1,0:T(8,128)(2,1)}, u32[]{:S(2)}) copy-start(bf16[256,4096]{1,0:T(8,128)(2,1)} %all-gather.2.cloned.1.call-done) | copy-start | bytes 6291460
Sparse Core Ops, SparseCore 0:
  42.9 32.1 all-gather.1
  81.4 58.8 reduce-scatter.1
where the time goes:
time: 150 us
  waiting for transfers between devices  84.4 us (56%)
  blocking collectives  32 us (21%)
  between operations  14.1 us (9%)
  matrix products  13.2 us (9%)
  local copies, waits for them, and re-layouts  4.15 us (3%)
  other arithmetic  1.78 us (1%)
    reduce_scatter x1, waiting for transfers between devices, per_device(): lax.psum_scatter(rounded.astype(jnp.bfloat16), 'dp', scatter_dimension=1,...  52.1 us
    all_gather x1, waiting for transfers between devices, per_device(): group_rows = lax.all_gather(incoming, 'ctx', axis=0, tiled=True)  32.3 us
    all_to_all x1, blocking collectives, per_device(): lax.all_to_all(outgoing, 'tp', split_axis=0, concat_axis=0, tiled=True)  32 us
    dot_general x1, matrix products, per_device(): jnp.einsum('rf,rd->fd', saved_rows, group_rows, preferred_element_type=jn...  6.12 us
    dot_general x1, matrix products, per_device(): jnp.einsum('rd,fd->rf', group_rows, weight, preferred_element_type=jnp.fl...  5.35 us
    unnamed x5, local copies, waits for them, and re-layouts  4.15 us
  transfers between devices with their start and end apart: 2, of which 2 were waited for; matrix products, arithmetic and copies ran while one was open for 4% of the time, Pallas kernels for 0%

commit v1 on v0

--- a/solution.py
+++ b/solution.py
@@ -1,10 +1,19 @@
+import functools
+
 import jax
 import jax.numpy as jnp
 from jax import lax
+from jax.experimental import pallas as pl
+from jax.experimental.pallas import tpu as pltpu
 from jax.sharding import PartitionSpec as P
 
-
-def per_device(out_grad, expert_ids, gate_weight, hidden_saved, down_weight):
+MESH = pl.DeviceIdType.MESH
+RELAY = ()
+ROWS_PER_TILE = 16
+LANES = 128
+
+
+def plain(out_grad, expert_ids, gate_weight, hidden_saved, down_weight):
     experts = lax.axis_size("tp")
     width = out_grad.shape[1]
     slots_all = hidden_saved.shape[2]
@@ -25,16 +34,254 @@
     outgoing = outgoing.reshape(experts, capacity, width)
     incoming = lax.all_to_all(outgoing, "tp", split_axis=0, concat_axis=0, tiled=True)
     incoming = incoming.reshape(experts * capacity, width)
-    weight = down_weight[0]
-    saved_rows = hidden_saved[0, 0]
     group_rows = lax.all_gather(incoming, "ctx", axis=0, tiled=True)
-    hidden_grad = jnp.einsum("rd,fd->rf", group_rows, weight, preferred_element_type=jnp.float32)
+    hidden_grad = jnp.einsum(
+        "rd,fd->rf", group_rows, down_weight[0], preferred_element_type=jnp.float32
+    )
     partial_value = jnp.einsum(
-        "rf,rd->fd", saved_rows, group_rows, preferred_element_type=jnp.float32
+        "rf,rd->fd", hidden_saved[0, 0], group_rows, preferred_element_type=jnp.float32
     )
     rounded = lax.optimization_barrier(partial_value.astype(jnp.bfloat16)).astype(jnp.float32)
     summed = lax.psum_scatter(rounded.astype(jnp.bfloat16), "dp", scatter_dimension=1, tiled=True)
     return (hidden_grad.astype(jnp.bfloat16)[None, None], summed[None])
+
+
+def kernel(
+    sizes, ids_ref, gate_ref, og_hbm, hs_hbm, dw_hbm, hg_ref, wg_ref,
+    ogb, wbuf, outb, disp, gath, hid, hgacc, wgacc,
+    load_sem, zs, zr, ys, yr, ps, pr, hs, hr,
+):
+    n_dp, n_ctx, n_tp, cap = sizes
+    half = n_dp // 2
+    rows = n_tp * cap
+    width = ogb.shape[2]
+    slots = n_ctx * rows
+    ff = hid.shape[2]
+    last = n_dp - 1
+    r, c, t = lax.axis_index("dp"), lax.axis_index("ctx"), lax.axis_index("tp")
+    hi, lo = r // 2, r % 2
+
+    steps = [(a, b) for a in range(1, half) for b in (0, 1)] + [(0, 1), (0, 0)]
+
+    def replica(a, b):
+        return lax.rem(hi + a, half) * 2 + lax.rem(lo + b, 2)
+
+    dest = [replica(a, b) for a, b in steps]
+
+    og_loads, w_loads = [], []
+    for k in range(n_dp):
+        cols = pl.ds(pl.multiple_of(dest[k] * width, LANES), width)
+        cp = pltpu.make_async_copy(og_hbm.at[:, cols], ogb.at[k], load_sem.at[0, k])
+        cp.start()
+        og_loads.append(cp)
+    hid_load = pltpu.make_async_copy(hs_hbm, hid.at[last], load_sem.at[2, 0])
+    hid_load.start()
+    for k in range(n_dp):
+        cols = pl.ds(pl.multiple_of(dest[k] * width, LANES), width)
+        cp = pltpu.make_async_copy(dw_hbm.at[:, cols], wbuf.at[k], load_sem.at[1, k])
+        cp.start()
+        w_loads.append(cp)
+
+    barrier = pltpu.get_barrier_semaphore()
+    peers = [(r, c, lax.rem(t + d, n_tp)) for d in range(1, n_tp)]
+    peers += [(r, lax.rem(c + d, n_ctx), t) for d in range(1, n_ctx)]
+    peers += [(dest[k], c, t) for k in range(n_dp - 1)]
+    for peer in peers:
+        pl.semaphore_signal(barrier, inc=1, device_id=peer, device_id_type=MESH)
+
+    tokens = ids_ref.shape[0]
+    lane = lax.broadcasted_iota(jnp.int32, (tokens, rows), 1)
+    lane_expert = lane // cap
+    lane_slot = (lane - lane_expert * cap).astype(jnp.float32)
+    mine = ids_ref[...] == lane_expert
+    onehot = jnp.where(mine, 1.0, 0.0)
+    earlier = (
+        lax.broadcasted_iota(jnp.int32, (tokens, tokens), 1)
+        < lax.broadcasted_iota(jnp.int32, (tokens, tokens), 0)
+    )
+    before = jnp.dot(
+        jnp.where(earlier, 1.0, 0.0).astype(jnp.bfloat16),
+        onehot.astype(jnp.bfloat16),
+        preferred_element_type=jnp.float32,
+    )
+    select = jnp.where(before == lane_slot, onehot, 0.0).T.astype(jnp.bfloat16)
+    gate = gate_ref[...]
+
+    started = []
+
+    def send(src, dst, ssem, rsem, device):
+        cp = pltpu.make_async_remote_copy(
+            src_ref=src, dst_ref=dst, send_sem=ssem, recv_sem=rsem,
+            device_id=device, device_id_type=MESH,
+        )
+        cp.start()
+        started.append(cp)
+        return cp
+
+    hid_recv = [None] * n_dp
+    z_recv = []
+    own_rows = pl.ds(pl.multiple_of(t * cap, cap), cap)
+    for k in range(n_dp):
+        og_loads[k].wait()
+        routed = (gate * ogb[k].astype(jnp.float32)).astype(jnp.bfloat16)
+        outb[k] = jnp.dot(select, routed, preferred_element_type=jnp.float32).astype(jnp.bfloat16)
+        if k == 0:
+            pl.semaphore_wait(barrier, len(peers))
+        copies = []
+        for d in range(1, n_tp):
+            to = lax.rem(t + d, n_tp)
+            src = outb.at[k, pl.ds(pl.multiple_of(to * cap, cap), cap)]
+            copies.append(
+                send(src, disp.at[k, c, own_rows], zs.at[k, d - 1], zr.at[k, d - 1], (r, c, to))
+            )
+        z_recv.append(copies)
+        disp[k, c, own_rows, :] = outb[k, own_rows, :]
+        if k == 0:
+            for a in range(1, half):
+                s = 2 * (a - 1)
+                hid_recv[s] = send(hs_hbm, hid.at[s], hs.at[s], hr.at[s], (dest[s], c, t))
+            s = n_dp - 2
+            hid_recv[s] = send(hs_hbm, hid.at[s], hs.at[s], hr.at[s], (dest[s], c, t))
+
+    y_recv = [None] * n_dp
+    p_recv = [[None] * n_ctx for _ in range(n_dp)]
+
+    def relay_hidden(a):
+        s = 2 * (a - 1)
+        hid_recv[s].wait_recv()
+        hid_recv[s + 1] = send(
+            hid.at[s], hid.at[s + 1], hs.at[s + 1], hr.at[s + 1], (dest[n_dp - 2], c, t)
+        )
+
+    def hidden_part(k):
+        w_loads[k].wait()
+        part = lax.dot_general(
+            disp[k].reshape(slots, width), wbuf[k], (((1,), (1,)), ((), ())),
+            preferred_element_type=jnp.float32,
+        )
+        if k == 0:
+            hgacc[...] = part
+        elif k < last:
+            hgacc[...] += part
+        else:
+            hg_ref[...] = (hgacc[...] + part).astype(hg_ref.dtype)
+
+    def weight_part(k, rows_in, first, final):
+        tile = 256 if ff % 256 == 0 else LANES
+        for f in range(0, ff, tile):
+            part = lax.dot_general(
+                hid[k, :, f : f + tile], rows_in, (((0,), (0,)), ((), ())),
+                preferred_element_type=jnp.float32,
+            )
+            if not first:
+                part = wgacc[f : f + tile, :] + part
+            if final:
+                wg_ref[f : f + tile, :] = part.astype(wg_ref.dtype)
+            else:
+                wgacc[f : f + tile, :] = part
+
+    def finish_y(k):
+        for d in range(1, n_ctx):
+            y_recv[k][d - 1].wait_recv()
+            if k < last and k not in RELAY:
+                other = lax.rem(c + d, n_ctx)
+                p_recv[k][d] = send(
+                    disp.at[k, other], gath.at[k, other], ps.at[k, d], pr.at[k, d], (dest[k], c, t)
+                )
+        hidden_part(k)
+
+    def relay_piece(k):
+        p_recv[k][0].wait_recv()
+        for d in range(1, n_ctx):
+            to = lax.rem(c + n_ctx - d, n_ctx)
+            p_recv[k][d] = send(gath.at[k, c], gath.at[k, c], ps.at[k, d], pr.at[k, d], (r, to, t))
+
+    for k in range(n_dp):
+        for cp in z_recv[k]:
+            cp.wait_recv()
+        y_recv[k] = []
+        if k < last:
+            p_recv[k][0] = send(
+                disp.at[k, c], gath.at[k, c], ps.at[k, 0], pr.at[k, 0], (dest[k], c, t)
+            )
+        for d in range(1, n_ctx):
+            to = lax.rem(c + n_ctx - d, n_ctx)
+            y_recv[k].append(
+                send(disp.at[k, c], disp.at[k, c], ys.at[k, d - 1], yr.at[k, d - 1], (r, to, t))
+            )
+        if k >= 1:
+            finish_y(k - 1)
+        if 1 <= k < half:
+            relay_hidden(k)
+        if k >= 2 and (k - 2) in RELAY:
+            relay_piece(k - 2)
+    for k in range(last - 1, last):
+        if k in RELAY:
+            relay_piece(k)
+    finish_y(last)
+
+    hid_load.wait()
+    weight_part(last, disp[last].reshape(slots, width), True, n_dp == 1)
+    arrive = [n_dp - 2] + list(range(n_dp - 2))
+    for at, k in enumerate(arrive):
+        if k >= n_dp - 2 or k % 2 == 1:
+            hid_recv[k].wait_recv()
+        for cp in p_recv[k][1:] if k in RELAY else p_recv[k]:
+            cp.wait_recv()
+        weight_part(k, gath[k].reshape(slots, width), False, at == len(arrive) - 1)
+    for cp in started:
+        cp.wait_send()
+
+
+def fused(sizes, out_grad, expert_ids, gate_weight, hidden_saved, down_weight):
+    n_dp, n_ctx, n_tp, cap = sizes
+    tokens, d_model = out_grad.shape
+    width = d_model // n_dp
+    rows = n_tp * cap
+    slots, ff = hidden_saved.shape[2:]
+    bf, dma = jnp.bfloat16, pltpu.SemaphoreType.DMA
+    vmem, hbm = pl.BlockSpec(memory_space=pltpu.VMEM), pl.BlockSpec(memory_space=pl.ANY)
+    hidden_grad, weight_grad = pl.pallas_call(
+        functools.partial(kernel, sizes),
+        out_shape=(
+            jax.ShapeDtypeStruct((slots, ff), bf),
+            jax.ShapeDtypeStruct((ff, width), bf),
+        ),
+        in_specs=[vmem, vmem, hbm, hbm, hbm],
+        out_specs=(vmem, vmem),
+        scratch_shapes=[
+            pltpu.VMEM((n_dp, tokens, width), bf),
+            pltpu.VMEM((n_dp, ff, width), bf),
+            pltpu.VMEM((n_dp, rows, width), bf),
+            pltpu.VMEM((n_dp, n_ctx, rows, width), bf),
+            pltpu.VMEM((n_dp - 1, n_ctx, rows, width), bf),
+            pltpu.VMEM((n_dp, slots, ff), bf),
+            pltpu.VMEM((slots, ff), jnp.float32),
+            pltpu.VMEM((ff, width), jnp.float32),
+            dma((3, n_dp)),
+            dma((n_dp, n_tp)),
+            dma((n_dp, n_tp)),
+            dma((n_dp, n_ctx)),
+            dma((n_dp, n_ctx)),
+            dma((n_dp, n_ctx)),
+            dma((n_dp, n_ctx)),
+            dma((n_dp,)),
+            dma((n_dp,)),
+        ],
+        compiler_params=pltpu.CompilerParams(collective_id=0, has_side_effects=True),
+    )(expert_ids, gate_weight, out_grad, hidden_saved[0, 0], down_weight[0])
+    return hidden_grad[None, None], weight_grad[None]
+
+
+def per_device(out_grad, expert_ids, gate_weight, hidden_saved, down_weight):
+    n_dp, n_ctx, n_tp = (lax.axis_size(name) for name in ("dp", "ctx", "tp"))
+    slots, ff = hidden_saved.shape[2:]
+    cap = slots // (n_ctx * n_tp)
+    args = (out_grad, expert_ids, gate_weight, hidden_saved, down_weight)
+    tiled = cap % ROWS_PER_TILE == 0 and ff % LANES == 0 and n_dp % 2 == 0
+    if tiled and out_grad.shape[1] % (n_dp * LANES) == 0:
+        return fused((n_dp, n_ctx, n_tp, cap), *args)
+    return plain(*args)
 
 
 def solution(mesh):

time: 150 us -> 54.5 us (0.36)
  waiting for transfers between devices: 84.4 us -> 0 us
  Pallas kernels: 0 us -> 45.6 us
  blocking collectives: 32 us -> 0 us
  between operations: 14.1 us -> 0.64 us
  matrix products: 13.2 us -> 0 us
  local copies, waits for them, and re-layouts: 4.15 us -> 7.21 us
  other arithmetic: 1.78 us -> 0 us
    reduce_scatter x1 -> x0, waiting for transfers between devices: 52.1 us -> none  [per_device(): lax.psum_scatter(rounded.astype(jnp.bfloat16), 'dp', scatter_dimension=1,...]
    pallas_call x0 -> x1, Pallas kernels: none -> 45.6 us  [fused(): pl.pallas_call(functools.partial(kernel, sizes), out_shape=(jax.ShapeDtyp...]
    all_gather x1 -> x0, waiting for transfers between devices: 32.3 us -> none  [per_device(): group_rows = lax.all_gather(incoming, 'ctx', axis=0, tiled=True)]
    all_to_all x1 -> x0, blocking collectives: 32 us -> none  [per_device(): lax.all_to_all(outgoing, 'tp', split_axis=0, concat_axis=0, tiled=True)]
    dot_general x3 -> x0, matrix products: 13.2 us -> none  [the longest x1 6.12 us: per_device(): jnp.einsum('rf,rd->fd', saved_rows, group_rows, preferred_element_type=jn...]
    unnamed x5 -> x4, local copies, waits for them, and re-layouts: 4.15 us -> 7.21 us
  transfers between devices with their start and end apart: 2 -> 0, of which waited for: 2 -> 0; matrix products, arithmetic and copies ran while one was open for 4% -> 0% of each run, Pallas kernels for 0% -> 0%
where the time goes in v1:
time: 54.5 us; the launch traced here: 53.5 us
  Pallas kernels  45.6 us (84%)
  local copies, waits for them, and re-layouts  7.21 us (13%)
  between operations  0.64 us (1%)
    pallas_call x1, Pallas kernels, fused(): pl.pallas_call(functools.partial(kernel, sizes), out_shape=(jax.ShapeDtyp...  45.6 us
    unnamed x4, local copies, waits for them, and re-layouts  7.21 us

profile of v1, /device:TPU:0, one launch (start us, length us, event | category | flops | bytes accessed | tf_op | source)
XLA Modules:
  0.0 53.5 jit_solution(2008646984587918225)
XLA Ops:
  0.6 1.4 %copy.7.ids_ref = s32[128,1]{1,0:T(8,128)} copy(s32[128,1]{0,1:T(1,128)} %param.6) | data formatting | bytes 1024 | tf_op args[1]
  2.0 1.4 %copy.8.gate_ref = f32[128,1]{1,0:T(8,128)} copy(f32[128,1]{0,1:T(1,128)} %param.7) | data formatting | bytes 1024 | tf_op args[2]
  3.4 45.6 %shard_map.68 = (bf16[256,768]{1,0:T(8,128)(2,1)}, bf16[768,1024]{1,0:T(8,128)(2,1)}) custom-call(s32[128,1]{1,0:T(8,128)} %copy.7.ids_ref, f32[128,1]{1,0:T(8,128)} %copy.8.gate_ref, bf16[128,4096]{1,0:T(8,128)(2,1)} %og_hbm.1, bf16[256,768]{1,0:T(8,128)(2,1)} %bitcast.7, bf16[768,4096]{1,0:T(8,128)(2,1)} %bitcast.4), custom_call_target="tpu_custom_call" | custom-call | tf_op jit(solution)/shard_map/pallas_call | solution.py:244
  49.0 1.8 %copy.11 = bf16[1,1,256,768]{3,2,1,0:T(8,128)(2,1)} copy(bf16[1,1,256,768]{3,2,1,0:T(8,128)(2,1)} %bitcast.6) | data formatting | bytes 786432
  50.8 2.7 %copy.12 = bf16[1,768,1024]{2,1,0:T(8,128)(2,1)} copy(bf16[1,768,1024]{2,1,0:T(8,128)(2,1)} %bitcast.5) | data formatting | bytes 3145728

commit v2 on v1

--- a/solution.py
+++ b/solution.py
@@ -89,23 +89,22 @@
     for peer in peers:
         pl.semaphore_signal(barrier, inc=1, device_id=peer, device_id_type=MESH)
 
-    tokens = ids_ref.shape[0]
-    lane = lax.broadcasted_iota(jnp.int32, (tokens, rows), 1)
-    lane_expert = lane // cap
-    lane_slot = (lane - lane_expert * cap).astype(jnp.float32)
-    mine = ids_ref[...] == lane_expert
-    onehot = jnp.where(mine, 1.0, 0.0)
+    tokens = ids_ref.shape[1]
+    row = lax.broadcasted_iota(jnp.int32, (rows, tokens), 0)
+    row_expert = row // cap
+    row_slot = (row - row_expert * cap).astype(jnp.float32)
+    onehot = jnp.where(ids_ref[...] == row_expert, 1.0, 0.0)
     earlier = (
-        lax.broadcasted_iota(jnp.int32, (tokens, tokens), 1)
-        < lax.broadcasted_iota(jnp.int32, (tokens, tokens), 0)
+        lax.broadcasted_iota(jnp.int32, (tokens, tokens), 0)
+        < lax.broadcasted_iota(jnp.int32, (tokens, tokens), 1)
     )
     before = jnp.dot(
+        onehot.astype(jnp.bfloat16),
         jnp.where(earlier, 1.0, 0.0).astype(jnp.bfloat16),
-        onehot.astype(jnp.bfloat16),
         preferred_element_type=jnp.float32,
     )
-    select = jnp.where(before == lane_slot, onehot, 0.0).T.astype(jnp.bfloat16)
-    gate = gate_ref[...]
+    select = jnp.where(before == row_slot, onehot, 0.0).astype(jnp.bfloat16)
+    gate = jnp.broadcast_to(gate_ref[...], (tokens, tokens)).T[:, :1]
 
     started = []
 
@@ -119,14 +118,15 @@
         return cp
 
     hid_recv = [None] * n_dp
+    pl.semaphore_wait(barrier, len(peers))
+    for s in [2 * a for a in range(half - 1)] + [n_dp - 2]:
+        hid_recv[s] = send(hs_hbm, hid.at[s], hs.at[s], hr.at[s], (dest[s], c, t))
     z_recv = []
     own_rows = pl.ds(pl.multiple_of(t * cap, cap), cap)
     for k in range(n_dp):
         og_loads[k].wait()
         routed = (gate * ogb[k].astype(jnp.float32)).astype(jnp.bfloat16)
         outb[k] = jnp.dot(select, routed, preferred_element_type=jnp.float32).astype(jnp.bfloat16)
-        if k == 0:
-            pl.semaphore_wait(barrier, len(peers))
         copies = []
         for d in range(1, n_tp):
             to = lax.rem(t + d, n_tp)
@@ -136,12 +136,6 @@
             )
         z_recv.append(copies)
         disp[k, c, own_rows, :] = outb[k, own_rows, :]
-        if k == 0:
-            for a in range(1, half):
-                s = 2 * (a - 1)
-                hid_recv[s] = send(hs_hbm, hid.at[s], hs.at[s], hr.at[s], (dest[s], c, t))
-            s = n_dp - 2
-            hid_recv[s] = send(hs_hbm, hid.at[s], hs.at[s], hr.at[s], (dest[s], c, t))
 
     y_recv = [None] * n_dp
     p_recv = [[None] * n_ctx for _ in range(n_dp)]
@@ -215,20 +209,26 @@
             relay_hidden(k)
         if k >= 2 and (k - 2) in RELAY:
             relay_piece(k - 2)
+    def weight_of(k, first, final):
+        if k == last:
+            hid_load.wait()
+            rows_in = disp[last]
+        else:
+            if k == last - 1 or k % 2 == 1:
+                hid_recv[k].wait_recv()
+            for cp in p_recv[k][1:] if k in RELAY else p_recv[k]:
+                cp.wait_recv()
+            rows_in = gath[k]
+        weight_part(k, rows_in.reshape(slots, width), first, final)
+
     for k in range(last - 1, last):
         if k in RELAY:
             relay_piece(k)
-    finish_y(last)
-
-    hid_load.wait()
-    weight_part(last, disp[last].reshape(slots, width), True, n_dp == 1)
-    arrive = [n_dp - 2] + list(range(n_dp - 2))
-    for at, k in enumerate(arrive):
-        if k >= n_dp - 2 or k % 2 == 1:
-            hid_recv[k].wait_recv()
-        for cp in p_recv[k][1:] if k in RELAY else p_recv[k]:
-            cp.wait_recv()
-        weight_part(k, gath[k].reshape(slots, width), False, at == len(arrive) - 1)
+    order = [0, last - 1, last] + list(range(1, last - 1))
+    for at, k in enumerate(order):
+        if k == last:
+            finish_y(last)
+        weight_of(k, at == 0, at == last)
     for cp in started:
         cp.wait_send()
 
@@ -269,7 +269,7 @@
             dma((n_dp,)),
         ],
         compiler_params=pltpu.CompilerParams(collective_id=0, has_side_effects=True),
-    )(expert_ids, gate_weight, out_grad, hidden_saved[0, 0], down_weight[0])
+    )(expert_ids.T, gate_weight.T, out_grad, hidden_saved[0, 0], down_weight[0])
     return hidden_grad[None, None], weight_grad[None]
 
 

time: 54.5 us -> 49.6 us (0.910)
  the two profiles are of different devices: /device:TPU:0 before, /device:TPU:8 now
where the time goes in v2:
time: 49.6 us; the launch traced here: 49.5 us
  Pallas kernels  44.4 us (90%)
  local copies, waits for them, and re-layouts  4.44 us (9%)
  between operations  0.64 us (1%)
    pallas_call x1, Pallas kernels, fused(): pl.pallas_call(functools.partial(kernel, sizes), out_shape=(jax.ShapeDtyp...  44.4 us
    unnamed x2, local copies, waits for them, and re-layouts  4.44 us

profile of v2, /device:TPU:8, one launch (start us, length us, event | category | flops | bytes accessed | tf_op | source)
XLA Modules:
  0.0 49.5 jit_solution(9141616131490515138)
XLA Ops:
  0.6 44.4 %shard_map.68 = (bf16[256,768]{1,0:T(8,128)(2,1)}, bf16[768,1024]{1,0:T(8,128)(2,1)}) custom-call(s32[1,128]{1,0:T(1,128)} %bitcast.10, f32[1,128]{1,0:T(1,128)} %bitcast.11, bf16[128,4096]{1,0:T(8,128)(2,1)} %og_hbm.1, bf16[256,768]{1,0:T(8,128)(2,1)} %bitcast.8, bf16[768,4096]{1,0:T(8,128)(2,1)} %bitcast.6), custom_call_target="tpu_custom_call" | custom-call | tf_op jit(solution)/shard_map/pallas_call | solution.py:244
  45.0 1.8 %copy.9 = bf16[1,1,256,768]{3,2,1,0:T(8,128)(2,1)} copy(bf16[1,1,256,768]{3,2,1,0:T(8,128)(2,1)} %bitcast.9) | data formatting | bytes 786432
  46.8 2.7 %copy.10 = bf16[1,768,1024]{2,1,0:T(8,128)(2,1)} copy(bf16[1,768,1024]{2,1,0:T(8,128)(2,1)} %bitcast.7) | data formatting | bytes 3145728

commit v3 on v2

--- a/solution.py
+++ b/solution.py
@@ -8,7 +8,8 @@
 from jax.sharding import PartitionSpec as P
 
 MESH = pl.DeviceIdType.MESH
-RELAY = ()
+RELAY = (1,)
+DIRECT = (1, 2)
 ROWS_PER_TILE = 16
 LANES = 128
 
@@ -48,8 +49,8 @@
 
 def kernel(
     sizes, ids_ref, gate_ref, og_hbm, hs_hbm, dw_hbm, hg_ref, wg_ref,
-    ogb, wbuf, outb, disp, gath, hid, hgacc, wgacc,
-    load_sem, zs, zr, ys, yr, ps, pr, hs, hr,
+    ogb, wbuf, outb, disp, gath, hid, hgacc, wgacc, hg_buf, wg_buf, out_sem,
+    load_sem, zs, zr, ys, yr, ps, pr, qs, qr, hs, hr,
 ):
     n_dp, n_ctx, n_tp, cap = sizes
     half = n_dp // 2
@@ -116,6 +117,15 @@
         cp.start()
         started.append(cp)
         return cp
+
+    y_recv = [[[] for _ in range(n_ctx)] for _ in range(n_dp)]
+
+    def share(k, src, part, at):
+        for d in range(1, n_ctx):
+            to = lax.rem(c + n_ctx - d, n_ctx)
+            y_recv[k][d].append(
+                send(src, disp.at[k, c, part], ys.at[k, d, at], yr.at[k, d, at], (r, to, t))
+            )
 
     hid_recv = [None] * n_dp
     pl.semaphore_wait(barrier, len(peers))
@@ -135,9 +145,11 @@
                 send(src, disp.at[k, c, own_rows], zs.at[k, d - 1], zr.at[k, d - 1], (r, c, to))
             )
         z_recv.append(copies)
+        share(k, outb.at[k, own_rows], own_rows, 0)
         disp[k, c, own_rows, :] = outb[k, own_rows, :]
 
-    y_recv = [None] * n_dp
+    out_copies, q_recv = [], []
+    cut = rows * DIRECT[0] // DIRECT[1]
     p_recv = [[None] * n_ctx for _ in range(n_dp)]
 
     def relay_hidden(a):
@@ -158,7 +170,9 @@
         elif k < last:
             hgacc[...] += part
         else:
-            hg_ref[...] = (hgacc[...] + part).astype(hg_ref.dtype)
+            hg_buf[...] = (hgacc[...] + part).astype(hg_buf.dtype)
+            out_copies.append(pltpu.make_async_copy(hg_buf, hg_ref, out_sem.at[0]))
+            out_copies[-1].start()
 
     def weight_part(k, rows_in, first, final):
         tile = 256 if ff % 256 == 0 else LANES
@@ -170,17 +184,26 @@
             if not first:
                 part = wgacc[f : f + tile, :] + part
             if final:
-                wg_ref[f : f + tile, :] = part.astype(wg_ref.dtype)
+                wg_buf[f : f + tile, :] = part.astype(wg_buf.dtype)
+                out_copies.append(
+                    pltpu.make_async_copy(
+                        wg_buf.at[f : f + tile], wg_ref.at[f : f + tile], out_sem.at[1 + f // tile]
+                    )
+                )
+                out_copies[-1].start()
             else:
                 wgacc[f : f + tile, :] = part
 
     def finish_y(k):
         for d in range(1, n_ctx):
-            y_recv[k][d - 1].wait_recv()
-            if k < last and k not in RELAY:
+            for cp in y_recv[k][d]:
+                cp.wait_recv()
+            if k < last:
                 other = lax.rem(c + d, n_ctx)
+                part = pl.ds(0, cut if k in RELAY else rows)
                 p_recv[k][d] = send(
-                    disp.at[k, other], gath.at[k, other], ps.at[k, d], pr.at[k, d], (dest[k], c, t)
+                    disp.at[k, other, part], gath.at[k, other, part], ps.at[k, d], pr.at[k, d],
+                    (dest[k], c, t),
                 )
         hidden_part(k)
 
@@ -188,20 +211,22 @@
         p_recv[k][0].wait_recv()
         for d in range(1, n_ctx):
             to = lax.rem(c + n_ctx - d, n_ctx)
-            p_recv[k][d] = send(gath.at[k, c], gath.at[k, c], ps.at[k, d], pr.at[k, d], (r, to, t))
+            part = pl.ds(cut, rows - cut)
+            q_recv.append(
+                send(
+                    gath.at[k, c, part], gath.at[k, c, part], qs.at[k, d], qr.at[k, d], (r, to, t)
+                )
+            )
 
     for k in range(n_dp):
-        for cp in z_recv[k]:
-            cp.wait_recv()
-        y_recv[k] = []
+        for d in range(1, n_tp):
+            z_recv[k][d - 1].wait_recv()
+            source = lax.rem(t + n_tp - d, n_tp)
+            part = pl.ds(pl.multiple_of(source * cap, cap), cap)
+            share(k, disp.at[k, c, part], part, d)
         if k < last:
             p_recv[k][0] = send(
                 disp.at[k, c], gath.at[k, c], ps.at[k, 0], pr.at[k, 0], (dest[k], c, t)
-            )
-        for d in range(1, n_ctx):
-            to = lax.rem(c + n_ctx - d, n_ctx)
-            y_recv[k].append(
-                send(disp.at[k, c], disp.at[k, c], ys.at[k, d - 1], yr.at[k, d - 1], (r, to, t))
             )
         if k >= 1:
             finish_y(k - 1)
@@ -216,7 +241,7 @@
         else:
             if k == last - 1 or k % 2 == 1:
                 hid_recv[k].wait_recv()
-            for cp in p_recv[k][1:] if k in RELAY else p_recv[k]:
+            for cp in p_recv[k][1:] + q_recv if k in RELAY else p_recv[k]:
                 cp.wait_recv()
             rows_in = gath[k]
         weight_part(k, rows_in.reshape(slots, width), first, final)
@@ -231,6 +256,8 @@
         weight_of(k, at == 0, at == last)
     for cp in started:
         cp.wait_send()
+    for cp in out_copies:
+        cp.wait()
 
 
 def fused(sizes, out_grad, expert_ids, gate_weight, hidden_saved, down_weight):
@@ -248,7 +275,7 @@
             jax.ShapeDtypeStruct((ff, width), bf),
         ),
         in_specs=[vmem, vmem, hbm, hbm, hbm],
-        out_specs=(vmem, vmem),
+        out_specs=(hbm, hbm),
         scratch_shapes=[
             pltpu.VMEM((n_dp, tokens, width), bf),
             pltpu.VMEM((n_dp, ff, width), bf),
@@ -258,9 +285,14 @@
             pltpu.VMEM((n_dp, slots, ff), bf),
             pltpu.VMEM((slots, ff), jnp.float32),
             pltpu.VMEM((ff, width), jnp.float32),
+            pltpu.VMEM((slots, ff), bf),
+            pltpu.VMEM((ff, width), bf),
+            dma((1 + ff // LANES,)),
             dma((3, n_dp)),
             dma((n_dp, n_tp)),
             dma((n_dp, n_tp)),
+            dma((n_dp, n_ctx, n_tp)),
+            dma((n_dp, n_ctx, n_tp)),
             dma((n_dp, n_ctx)),
             dma((n_dp, n_ctx)),
             dma((n_dp, n_ctx)),
@@ -270,7 +302,43 @@
         ],
         compiler_params=pltpu.CompilerParams(collective_id=0, has_side_effects=True),
     )(expert_ids.T, gate_weight.T, out_grad, hidden_saved[0, 0], down_weight[0])
+    hidden_grad, weight_grad = settle(hidden_grad, weight_grad)
     return hidden_grad[None, None], weight_grad[None]
+
+
+def settle_kernel(pieces, a_ref, b_ref, a_out, b_out, a_buf, b_buf, in_sem, out_sem):
+    moves = [(a_ref, a_buf, a_out, 0, a_ref.shape[0])]
+    size = b_ref.shape[0] // pieces
+    moves += [(b_ref, b_buf, b_out, p * size, size) for p in range(pieces)]
+    loads, stores = [], []
+    for i, (src, buf, _, start, length) in enumerate(moves):
+        part = pl.ds(start, length)
+        loads.append(pltpu.make_async_copy(src.at[part], buf.at[part], in_sem.at[i]))
+        loads[-1].start()
+    for i, (_, buf, dst, start, length) in enumerate(moves):
+        part = pl.ds(start, length)
+        loads[i].wait()
+        stores.append(pltpu.make_async_copy(buf.at[part], dst.at[part], out_sem.at[i]))
+        stores[-1].start()
+    for cp in stores:
+        cp.wait()
+
+
+def settle(a, b):
+    pieces = 4 if b.shape[0] % (4 * ROWS_PER_TILE) == 0 else 1
+    hbm = pl.BlockSpec(memory_space=pl.ANY)
+    return pl.pallas_call(
+        functools.partial(settle_kernel, pieces),
+        out_shape=tuple(jax.ShapeDtypeStruct(x.shape, x.dtype) for x in (a, b)),
+        in_specs=[hbm, hbm],
+        out_specs=(hbm, hbm),
+        scratch_shapes=[
+            pltpu.VMEM(a.shape, a.dtype),
+            pltpu.VMEM(b.shape, b.dtype),
+            pltpu.SemaphoreType.DMA((pieces + 1,)),
+            pltpu.SemaphoreType.DMA((pieces + 1,)),
+        ],
+    )(a, b)
 
 
 def per_device(out_grad, expert_ids, gate_weight, hidden_saved, down_weight):

time: 49.6 us -> 44.4 us (0.90)
  the two profiles are of different devices: /device:TPU:8 before, /device:TPU:0 now
where the time goes in v3:
time: 44.4 us; the launch traced here: 44.2 us
  Pallas kernels  43.6 us (98%)
  between operations  0.64 us (1%)
    pallas_call x1, Pallas kernels, fused(): pl.pallas_call(functools.partial(kernel, sizes), out_shape=(jax.ShapeDtyp...  41.2 us
    pallas_call x1, Pallas kernels, settle(): pl.pallas_call(functools.partial(settle_kernel, pieces), out_shape=tuple(...  2.35 us

profile of v3, /device:TPU:0, one launch (start us, length us, event | category | flops | bytes accessed | tf_op | source)
XLA Modules:
  0.0 44.2 jit_solution(11088972755510472611)
XLA Ops:
  0.6 41.2 %shard_map.68 = (bf16[256,768]{1,0:T(8,128)(2,1)}, bf16[768,1024]{1,0:T(8,128)(2,1)}) custom-call(s32[1,128]{1,0:T(1,128)} %bitcast.8, f32[1,128]{1,0:T(1,128)} %bitcast.9, bf16[128,4096]{1,0:T(8,128)(2,1)} %og_hbm.1, bf16[256,768]{1,0:T(8,128)(2,1)} %bitcast.7, bf16[768,4096]{1,0:T(8,128)(2,1)} %bitcast.6), custom_call_target="tpu_custom_call" | custom-call | tf_op jit(solution)/shard_map/pallas_call | solution.py:271
  41.9 2.3 %shard_map.69 = (bf16[256,768]{1,0:T(8,128)(2,1)}, bf16[768,1024]{1,0:T(8,128)(2,1)}) custom-call(bf16[256,768]{1,0:T(8,128)(2,1)} %get-tuple-element.6.a_ref, bf16[768,1024]{1,0:T(8,128)(2,1)} %get-tuple-element.7.b_ref), custom_call_target="tpu_custom_call" | custom-call | tf_op jit(solution)/shard_map/pallas_call | solution.py:330

commit v4 on v3

--- a/solution.py
+++ b/solution.py
@@ -50,7 +50,7 @@
 def kernel(
     sizes, ids_ref, gate_ref, og_hbm, hs_hbm, dw_hbm, hg_ref, wg_ref,
     ogb, wbuf, outb, disp, gath, hid, hgacc, wgacc, hg_buf, wg_buf, out_sem,
-    load_sem, zs, zr, ys, yr, ps, pr, qs, qr, hs, hr,
+    load_sem, zs, zr, ys, yr, ps, pr, qs, qr, hs, hr, gs, gr,
 ):
     n_dp, n_ctx, n_tp, cap = sizes
     half = n_dp // 2
@@ -126,6 +126,13 @@
             y_recv[k][d].append(
                 send(src, disp.at[k, c, part], ys.at[k, d, at], yr.at[k, d, at], (r, to, t))
             )
+
+    g_recv = [[] for _ in range(n_dp)]
+
+    def give(k, src, part, at):
+        g_recv[k].append(
+            send(src, gath.at[k, c, part], gs.at[k, at], gr.at[k, at], (dest[k], c, t))
+        )
 
     hid_recv = [None] * n_dp
     pl.semaphore_wait(barrier, len(peers))
@@ -146,6 +153,8 @@
             )
         z_recv.append(copies)
         share(k, outb.at[k, own_rows], own_rows, 0)
+        if k < last:
+            give(k, outb.at[k, own_rows], own_rows, 0)
         disp[k, c, own_rows, :] = outb[k, own_rows, :]
 
     out_copies, q_recv = [], []
@@ -208,7 +217,8 @@
         hidden_part(k)
 
     def relay_piece(k):
-        p_recv[k][0].wait_recv()
+        for cp in g_recv[k]:
+            cp.wait_recv()
         for d in range(1, n_ctx):
             to = lax.rem(c + n_ctx - d, n_ctx)
             part = pl.ds(cut, rows - cut)
@@ -224,16 +234,14 @@
             source = lax.rem(t + n_tp - d, n_tp)
             part = pl.ds(pl.multiple_of(source * cap, cap), cap)
             share(k, disp.at[k, c, part], part, d)
-        if k < last:
-            p_recv[k][0] = send(
-                disp.at[k, c], gath.at[k, c], ps.at[k, 0], pr.at[k, 0], (dest[k], c, t)
-            )
+            if k < last:
+                give(k, disp.at[k, c, part], part, d)
+        if k >= 2 and (k - 2) in RELAY:
+            relay_piece(k - 2)
         if k >= 1:
             finish_y(k - 1)
         if 1 <= k < half:
             relay_hidden(k)
-        if k >= 2 and (k - 2) in RELAY:
-            relay_piece(k - 2)
     def weight_of(k, first, final):
         if k == last:
             hid_load.wait()
@@ -241,7 +249,8 @@
         else:
             if k == last - 1 or k % 2 == 1:
                 hid_recv[k].wait_recv()
-            for cp in p_recv[k][1:] + q_recv if k in RELAY else p_recv[k]:
+            extra = q_recv if k in RELAY else g_recv[k]
+            for cp in p_recv[k][1:] + extra:
                 cp.wait_recv()
             rows_in = gath[k]
         weight_part(k, rows_in.reshape(slots, width), first, final)
@@ -299,6 +308,8 @@
             dma((n_dp, n_ctx)),
             dma((n_dp,)),
             dma((n_dp,)),
+            dma((n_dp, n_tp)),
+            dma((n_dp, n_tp)),
         ],
         compiler_params=pltpu.CompilerParams(collective_id=0, has_side_effects=True),
     )(expert_ids.T, gate_weight.T, out_grad, hidden_saved[0, 0], down_weight[0])

time: 44.4 us -> 44.4 us (level)
  no operation moved by 1% of the time
where the time goes in v4:
time: 44.4 us; the launch traced here: 44.2 us
  Pallas kernels  43.6 us (98%)
  between operations  0.64 us (1%)
    pallas_call x1, Pallas kernels, fused(): pl.pallas_call(functools.partial(kernel, sizes), out_shape=(jax.ShapeDtyp...  41.2 us
    pallas_call x1, Pallas kernels, settle(): pl.pallas_call(functools.partial(settle_kernel, pieces), out_shape=tuple(...  2.35 us

profile of v4, /device:TPU:0, one launch (start us, length us, event | category | flops | bytes accessed | tf_op | source)
XLA Modules:
  0.0 44.2 jit_solution(14356737208407265548)
XLA Ops:
  0.6 41.2 %shard_map.68 = (bf16[256,768]{1,0:T(8,128)(2,1)}, bf16[768,1024]{1,0:T(8,128)(2,1)}) custom-call(s32[1,128]{1,0:T(1,128)} %bitcast.8, f32[1,128]{1,0:T(1,128)} %bitcast.9, bf16[128,4096]{1,0:T(8,128)(2,1)} %og_hbm.1, bf16[256,768]{1,0:T(8,128)(2,1)} %bitcast.7, bf16[768,4096]{1,0:T(8,128)(2,1)} %bitcast.6), custom_call_target="tpu_custom_call" | custom-call | tf_op jit(solution)/shard_map/pallas_call | solution.py:280
  41.9 2.3 %shard_map.69 = (bf16[256,768]{1,0:T(8,128)(2,1)}, bf16[768,1024]{1,0:T(8,128)(2,1)}) custom-call(bf16[256,768]{1,0:T(8,128)(2,1)} %get-tuple-element.6.a_ref, bf16[768,1024]{1,0:T(8,128)(2,1)} %get-tuple-element.7.b_ref), custom_call_target="tpu_custom_call" | custom-call | tf_op jit(solution)/shard_map/pallas_call | solution.py:341
